TPU v7x, 32 devices: a whole 2x2x4 slice. The times are simulated.
32 devices in a mesh: ctx: 4 (over y, x), grp: 4 (over z), side: 2 (over core).
Axes of the slice: x: 2, y: 2, z: 4, core: 2. Of those that a mesh axis runs over, the one named last changes fastest.
Arguments:
- tokens: bfloat16 [512, 2048], P(('ctx', 'grp', 'side')), may hold values from -6 to 6
- norm_gain: float32 [2048], replicated, may hold values from 0.25 to 1.75
- combine: float32 [512, 8], P(('ctx', 'grp', 'side')), may hold values from 0.05 to 0.6
- expert_ids: int32 [512, 8], P(('ctx', 'grp', 'side')), may hold values from 0 to 15, all different within a row; in each aligned block of 16 rows (0 to 15, 16 to 31, ...) at most 11 rows name the same one
- w_gate: bfloat16 [16, 2048, 768], P(('ctx', 'grp'), None, 'side'), may hold values from -0.125 to 0.125
- w_up: bfloat16 [16, 2048, 768], P(('ctx', 'grp'), None, 'side'), may hold values from -0.125 to 0.125
- w_down: bfloat16 [16, 768, 2048], P(('ctx', 'grp'), 'side'), may hold values from -0.21875 to 0.21875
- d_out: bfloat16 [512, 2048], P(('ctx', 'grp', 'side')), may hold values from -6 to 6
Outputs:
- mixed: bfloat16 [512, 2048], P(('ctx', 'grp', 'side'))
- d_tokens: bfloat16 [512, 2048], P(('ctx', 'grp', 'side'))
- d_gain: float32 [2048], replicated
- d_combine: float32 [512, 8], P(('ctx', 'grp', 'side'))
- d_w_gate: bfloat16 [16, 2048, 768], P(('ctx', 'grp'), None, 'side')
- d_w_up: bfloat16 [16, 2048, 768], P(('ctx', 'grp'), None, 'side')
- d_w_down: bfloat16 [16, 768, 2048], P(('ctx', 'grp'), 'side')
Inputs may be any that keep to these rules, and one draw needn't show every extreme that they name: `expert_ids`: each row names 8 different experts; among the 16 rows of one device no expert is named more than 11 times, and that bound is reached.
All inputs are finite; a program needn't handle non-finite values.
Results may differ from a plain program's by a relative error of at most 0.0072.
Values may be sent and summed in bfloat16 or wider, within the bound.
A program may use at most 128 MiB of HBM per device.

v0:
```python
import jax
import jax.numpy as jnp
from jax import lax
from jax.sharding import PartitionSpec as P

EPS = 1e-06


def expert_pass(rows, grads, gate_w, up_w, down_w):
    a_gate = jnp.dot(rows, gate_w, preferred_element_type=jnp.float32)
    a_up = jnp.dot(rows, up_w, preferred_element_type=jnp.float32)
    sigmoid_gate = jax.nn.sigmoid(a_gate)
    silu_gate = a_gate * sigmoid_gate
    hidden = (silu_gate * a_up).astype(jnp.bfloat16)
    output = jnp.dot(hidden, down_w, preferred_element_type=jnp.float32)
    d_hidden = lax.dot_general(
        grads, down_w, (((1,), (1,)), ((), ())), preferred_element_type=jnp.float32
    )
    d_up = (d_hidden * silu_gate).astype(jnp.bfloat16)
    d_gate = (d_hidden * a_up * sigmoid_gate * (1.0 + a_gate * (1.0 - sigmoid_gate))).astype(
        jnp.bfloat16
    )
    d_rows = lax.dot_general(
        d_gate, gate_w, (((1,), (1,)), ((), ())), preferred_element_type=jnp.float32
    )
    d_rows = d_rows + lax.dot_general(
        d_up, up_w, (((1,), (1,)), ((), ())), preferred_element_type=jnp.float32
    )
    g_gate = lax.dot_general(
        rows, d_gate, (((0,), (0,)), ((), ())), preferred_element_type=jnp.float32
    )
    g_up = lax.dot_general(rows, d_up, (((0,), (0,)), ((), ())), preferred_element_type=jnp.float32)
    g_down = lax.dot_general(
        hidden, grads, (((0,), (0,)), ((), ())), preferred_element_type=jnp.float32
    )
    return (output, d_rows, g_gate, g_up, g_down)


def local(tokens, norm_gain, combine, expert_ids, w_gate, w_up, w_down, d_out):
    count = tokens.shape[0]
    width = tokens.shape[1]
    chosen = expert_ids.shape[1]
    n_ctx = lax.axis_size("ctx")
    n_grp = lax.axis_size("grp")
    experts = n_ctx * n_grp
    slots = max(2, (4 * count * chosen + 3 * experts - 1) // (3 * experts))
    places = experts * slots
    x_float = tokens.astype(jnp.float32)
    inv_rms = lax.rsqrt(jnp.mean(x_float * x_float, axis=1, keepdims=True) + EPS)
    normed = (x_float * inv_rms * norm_gain).astype(jnp.bfloat16)
    grad_float = d_out.astype(jnp.float32)
    flat_ids = expert_ids.reshape(-1)
    onehot = (flat_ids[:, None] == jnp.arange(experts, dtype=jnp.int32)[None, :]).astype(jnp.int32)
    before = jnp.cumsum(onehot, axis=0) - onehot
    slot = jnp.sum(before * onehot, axis=1)
    target = flat_ids * slots + slot
    select = (target[:, None] == jnp.arange(places, dtype=jnp.int32)[None, :]).astype(jnp.float32)
    per_token = select.reshape(count, chosen, places)
    token_map = jnp.sum(per_token, axis=1).astype(jnp.bfloat16)
    weighted = jnp.sum(per_token * combine[:, :, None], axis=1)
    send_rows = lax.dot_general(
        token_map, normed, (((0,), (0,)), ((), ())), preferred_element_type=jnp.float32
    ).astype(jnp.bfloat16)
    send_grads = lax.dot_general(
        weighted,
        grad_float,
        (((0,), (0,)), ((), ())),
        precision=lax.Precision.HIGHEST,
        preferred_element_type=jnp.float32,
    ).astype(jnp.bfloat16)
    rows_in, grads_in = (
        lax.all_to_all(
            send_rows.reshape(experts, slots, width),
            ("ctx", "grp"),
            split_axis=0,
            concat_axis=0,
            tiled=True,
        ),
        lax.all_to_all(
            send_grads.reshape(experts, slots, width),
            ("ctx", "grp"),
            split_axis=0,
            concat_axis=0,
            tiled=True,
        ),
    )
    full_gate, full_up, full_down = (
        lax.all_gather(w_gate[0], "side", axis=1, tiled=True),
        lax.all_gather(w_up[0], "side", axis=1, tiled=True),
        lax.all_gather(w_down[0], "side", axis=0, tiled=True),
    )
    output, d_rows, g_gate, g_up, g_down = expert_pass(
        rows_in.reshape(places, width),
        grads_in.reshape(places, width),
        full_gate,
        full_up,
        full_down,
    )
    own_gate, own_up, own_down = (
        lax.psum_scatter(g_gate, "side", scatter_dimension=1, tiled=True),
        lax.psum_scatter(g_up, "side", scatter_dimension=1, tiled=True),
        lax.psum_scatter(g_down, "side", scatter_dimension=0, tiled=True),
    )
    back_out = output.astype(jnp.bfloat16)
    back_rows = d_rows.astype(jnp.bfloat16)
    came_out, came_rows = (
        lax.all_to_all(
            back_out.reshape(experts, slots, width),
            ("ctx", "grp"),
            split_axis=0,
            concat_axis=0,
            tiled=True,
        ),
        lax.all_to_all(
            back_rows.reshape(experts, slots, width),
            ("ctx", "grp"),
            split_axis=0,
            concat_axis=0,
            tiled=True,
        ),
    )
    slot_out = jnp.dot(
        select.astype(jnp.bfloat16),
        came_out.reshape(places, width),
        preferred_element_type=jnp.float32,
    ).reshape(count, chosen, width)
    mixed = (x_float + jnp.sum(combine[:, :, None] * slot_out, axis=1)).astype(jnp.bfloat16)
    d_combine = jnp.einsum("tkd,td->tk", slot_out, grad_float, precision=lax.Precision.HIGHEST)
    d_normed = jnp.dot(
        token_map, came_rows.reshape(places, width), preferred_element_type=jnp.float32
    )
    d_gain = lax.psum(jnp.sum(d_normed * x_float * inv_rms, axis=0), ("ctx", "grp", "side"))
    scaled = d_normed * norm_gain
    d_tokens = (
        grad_float
        + inv_rms * scaled
        - x_float * inv_rms**3 * jnp.mean(scaled * x_float, axis=1, keepdims=True)
    )
    return (
        mixed,
        d_tokens.astype(jnp.bfloat16),
        d_gain,
        d_combine,
        own_gate.astype(jnp.bfloat16)[None],
        own_up.astype(jnp.bfloat16)[None],
        own_down.astype(jnp.bfloat16)[None],
    )


def solution(mesh):
    in_specs = (
        P(("ctx", "grp", "side"), None),
        P(),
        P(("ctx", "grp", "side"), None),
        P(("ctx", "grp", "side"), None),
        P(("ctx", "grp"), None, "side"),
        P(("ctx", "grp"), None, "side"),
        P(("ctx", "grp"), "side", None),
        P(("ctx", "grp", "side"), None),
    )
    out_specs = (
        P(("ctx", "grp", "side"), None),
        P(("ctx", "grp", "side"), None),
        P(),
        P(("ctx", "grp", "side"), None),
        P(("ctx", "grp"), None, "side"),
        P(("ctx", "grp"), None, "side"),
        P(("ctx", "grp"), "side", None),
    )
    return jax.shard_map(local, mesh=mesh, in_specs=in_specs, out_specs=out_specs, check_vma=False)
```

profile of v0, /device:TPU:12, one launch (start us, length us, event | category | flops | bytes accessed | tf_op | source)
XLA Modules:
  0.0 222.5 jit_solution(12201147010498002594)
XLA Ops:
  7.2 0.0 all-gather.11.cloned.1.call-start
  7.2 0.7 all-gather.11.cloned.1.call-update
  7.9 0.0 all-gather.9.cloned.1.call-start
  8.0 0.7 all-gather.9.cloned.1.call-update
  8.7 0.1 copy.23
  8.8 0.1 copy.24
  8.8 0.1 eq.49
  8.9 0.1 fusion.41
  9.0 0.2 reduce_window_sum.11
  9.2 0.2 select_reduce_fusion.1
  9.4 0.1 reduce_sum.66
  9.5 0.0 copy-start.10
  9.5 0.0 copy-start.6
  9.5 0.2 select_reduce_fusion
  9.7 0.0 copy-start.7
  9.7 0.8 convolution_convert_fusion
  10.5 1.2 reshape.111
  11.7 7.2 %all-to-all-start.2 = ((bf16[16,11,2048]{2,1,0:T(8,128)(2,1)}), bf16[16,11,2048]{2,1,0:T(8,128)(2,1)S(1)}, u32[]{:S(2)}, u32[]{:S(2)}) async-start(bf16[16,11,2048]{2,1,0:T(8,128)(2,1)} %reshape.111), calls=%async_computation.2 | async-start | bytes 2097152 | tf_op jit(solution)/shard_map/all_to_all | solution.py:79
  18.9 0.0 all-gather.7.cloned.1.call-start
  18.9 0.7 all-gather.7.cloned.1.call-update
  19.6 0.1 fusion.22
  19.8 0.5 multiply_multiply_fusion
  20.3 0.4 convolution_convert_fusion.1
  20.7 1.2 reshape.107
  21.9 20.6 %all-to-all-done.2 = bf16[16,11,2048]{2,1,0:T(8,128)(2,1)S(1)} async-done(((bf16[16,11,2048]{2,1,0:T(8,128)(2,1)}), bf16[16,11,2048]{2,1,0:T(8,128)(2,1)S(1)}, u32[]{:S(2)}, u32[]{:S(2)}) %all-to-all-start.2) | async-done | bytes 720928 | tf_op jit(solution)/shard_map/all_to_all | solution.py:79
  42.5 7.5 %all-to-all-start = ((bf16[16,11,2048]{2,1,0:T(8,128)(2,1)}), bf16[16,11,2048]{2,1,0:T(8,128)(2,1)S(1)}, u32[]{:S(2)}, u32[]{:S(2)}) async-start(bf16[16,11,2048]{2,1,0:T(8,128)(2,1)} %reshape.107), calls=%async_computation | async-start | bytes 2097152 | tf_op jit(solution)/shard_map/all_to_all | solution.py:72
  49.9 0.0 reduce-scatter.8.cloned.1.call-start
  50.0 0.3 reshape.112
  50.3 22.6 %all-to-all-done = bf16[16,11,2048]{2,1,0:T(8,128)(2,1)S(1)} async-done(((bf16[16,11,2048]{2,1,0:T(8,128)(2,1)}), bf16[16,11,2048]{2,1,0:T(8,128)(2,1)S(1)}, u32[]{:S(2)}, u32[]{:S(2)}) %all-to-all-start) | async-done | bytes 720928 | tf_op jit(solution)/shard_map/all_to_all | solution.py:72
  72.9 0.3 reshape.108
  73.2 0.0 all-gather.11.cloned.1.call-done
  73.2 3.1 %fusion = f32[176,768]{1,0:T(8,128)S(1)} fusion(bf16[176,2048]{1,0:T(8,128)(2,1)S(1)} %reshape.112, bf16[1,768,2048]{2,1,0:T(8,128)(2,1)} %all-gather.11.cloned.1.call-done), kind=kOutput, calls=%fused_computation | convolution fusion | flops 553648128 | bytes 4407296 | tf_op jit(solution)/shard_map/dot_general | solution.py:16
  76.3 0.0 all-gather.9.cloned.1.call-done
  76.4 2.6 %fusion.6 = f32[176,768]{1,0:T(8,128)S(1)} fusion(bf16[176,2048]{1,0:T(8,128)(2,1)S(1)} %reshape.108, bf16[1,2048,768]{2,1,0:T(8,128)(2,1)} %all-gather.9.cloned.1.call-done), kind=kOutput, calls=%fused_computation.6 | convolution fusion | flops 553648128 | bytes 4407296 | tf_op jit(solution)/shard_map/dot_general | solution.py:11
  79.0 0.0 all-gather.7.cloned.1.call-done
  79.0 2.8 %multiply_convert_fusion.1 = (bf16[176,768]{1,0:T(8,128)(2,1)S(1)}, bf16[176,768]{1,0:T(8,128)(2,1)S(1)}, bf16[176,768]{1,0:T(8,128)(2,1)S(1)}) fusion(f32[176,768]{1,0:T(8,128)S(1)} %fusion, f32[176,768]{1,0:T(8,128)S(1)} %fusion.6, bf16[176,2048]{1,0:T(8,128)(2,1)S(1)} %reshape.108, bf16[1,2048,768]{2,1,0:T(8,128)(2,1)} %all-gather.7.cloned.1.call-done), kind=kOutput, calls=%fused_computation.22 | convolution fusion | flops 555675648 | bytes 5758976 | tf_op jit(solution)/shard_map/dot_general | solution.py:10
  81.8 3.6 %fusion.47 = f32[768,2048]{1,0:T(8,128)} fusion(bf16[176,768]{1,0:T(8,128)(2,1)S(1)} %get-tuple-element.13, bf16[176,2048]{1,0:T(8,128)(2,1)S(1)} %reshape.112), kind=kOutput, calls=%fused_computation.66 | convolution fusion | flops 553648128 | bytes 7282688 | tf_op jit(solution)/shard_map/dot_general | solution.py:33
  85.5 0.0 reduce-scatter.8.cloned.1.call-update
  85.5 0.0 reduce-scatter.4.cloned.1.call-start
  85.5 3.7 %fusion.45 = f32[2048,768]{1,0:T(8,128)} fusion(bf16[176,2048]{1,0:T(8,128)(2,1)S(1)} %reshape.108, bf16[176,768]{1,0:T(8,128)(2,1)S(1)} %get-tuple-element.11), kind=kOutput, calls=%fused_computation.64 | convolution fusion | flops 553648128 | bytes 7282688 | tf_op jit(solution)/shard_map/dot_general | solution.py:29
  89.2 0.0 reduce-scatter.4.cloned.1.call-update
  89.3 0.0 reduce-scatter.6.cloned.1.call-start
  89.3 4.0 %fusion.46 = f32[2048,768]{1,0:T(8,128)} fusion(bf16[176,2048]{1,0:T(8,128)(2,1)S(1)} %reshape.108, bf16[176,768]{1,0:T(8,128)(2,1)S(1)} %get-tuple-element.12), kind=kOutput, calls=%fused_computation.65 | convolution fusion | flops 553648128 | bytes 7282688 | tf_op jit(solution)/shard_map/dot_general | solution.py:32
  93.3 0.0 reduce-scatter.6.cloned.1.call-update
  93.4 3.7 %fusion.15 = bf16[176,2048]{1,0:T(8,128)(2,1)} fusion(bf16[176,768]{1,0:T(8,128)(2,1)S(1)} %get-tuple-element.13, bf16[1,768,2048]{2,1,0:T(8,128)(2,1)} %all-gather.11.cloned.1.call-done), kind=kOutput, calls=%fused_computation.13 | convolution fusion | flops 554008576 | bytes 4136960 | tf_op jit(solution)/shard_map/dot_general | solution.py:15
  97.1 2.6 %reshape.109 = bf16[16,11,2048]{2,1,0:T(8,128)(2,1)} reshape(bf16[176,2048]{1,0:T(8,128)(2,1)} %fusion.15) | data formatting | bytes 1441792 | tf_op jit(solution)/shard_map/reshape | solution.py:108
  99.6 9.3 %all-to-all-start.1 = ((bf16[16,11,2048]{2,1,0:T(8,128)(2,1)}), bf16[16,11,2048]{2,1,0:T(8,128)(2,1)}, u32[]{:S(2)}, u32[]{:S(2)}) async-start(bf16[16,11,2048]{2,1,0:T(8,128)(2,1)} %reshape.109), calls=%async_computation.1 | async-start | bytes 2097152 | tf_op jit(solution)/shard_map/all_to_all | solution.py:107
  108.9 2.3 %fusion.4 = f32[176,2048]{1,0:T(8,128)S(1)} fusion(bf16[176,768]{1,0:T(8,128)(2,1)} %copy-done.4, bf16[1,2048,768]{2,1,0:T(8,128)(2,1)S(1)} %copy-done), kind=kOutput, calls=%fused_computation.4 | convolution fusion | flops 553648128 | bytes 4857856 | tf_op jit(solution)/shard_map/dot_general | solution.py:26
  111.2 1.2 fusion.18
  112.4 1.2 reshape.113
  113.7 17.7 %all-to-all-done.1 = bf16[16,11,2048]{2,1,0:T(8,128)(2,1)} async-done(((bf16[16,11,2048]{2,1,0:T(8,128)(2,1)}), bf16[16,11,2048]{2,1,0:T(8,128)(2,1)}, u32[]{:S(2)}, u32[]{:S(2)}) %all-to-all-start.1) | async-done | bytes 720928 | tf_op jit(solution)/shard_map/all_to_all | solution.py:107
  131.4 7.5 %all-to-all-start.3 = ((bf16[16,11,2048]{2,1,0:T(8,128)(2,1)}), bf16[16,11,2048]{2,1,0:T(8,128)(2,1)S(1)}, u32[]{:S(2)}, u32[]{:S(2)}) async-start(bf16[16,11,2048]{2,1,0:T(8,128)(2,1)} %reshape.113), calls=%async_computation.3 | async-start | bytes 2097152 | tf_op jit(solution)/shard_map/all_to_all | solution.py:114
  138.9 1.5 reshape.118
  140.4 0.5 multiply_reduce_fusion
  140.9 1.1 fusion.32
  142.1 0.7 copy.28
  142.8 19.0 %all-to-all-done.3 = bf16[16,11,2048]{2,1,0:T(8,128)(2,1)S(1)} async-done(((bf16[16,11,2048]{2,1,0:T(8,128)(2,1)}), bf16[16,11,2048]{2,1,0:T(8,128)(2,1)S(1)}, u32[]{:S(2)}, u32[]{:S(2)}) %all-to-all-start.3) | async-done | bytes 720928 | tf_op jit(solution)/shard_map/all_to_all | solution.py:114
  161.8 0.3 reshape.114
  162.1 0.3 fusion.31
  162.4 42.8 %psum.7 = f32[2048]{0:T(1024)} all-reduce(f32[2048]{0:T(1024)S(1)} %get-tuple-element.7), channel_id=1, replica_groups=mesh['ctx'=4,'grp'=4,'side'=2] {'ctx','grp','side'}, use_global_device_ids=true, to_apply=%region_8.9 | all-reduce | flops 2048 | bytes 16384 | tf_op jit(solution)/shard_map/psum | solution.py:132
  205.2 0.7 fusion.28
  206.0 3.3 %convert_bitcast_fusion = bf16[1,384,2048]{2,1,0:T(8,128)(2,1)} fusion(f32[384,2048]{1,0:T(8,128)} %reduce-scatter.8.cloned.1.call-done), kind=kLoop, calls=%fused_computation.17 | loop fusion | flops 786432 | bytes 4718592 | tf_op jit(solution)/shard_map/broadcast_in_dim | solution.py:146
  209.2 3.2 %convert_bitcast_fusion.2 = bf16[1,2048,384]{2,1,0:T(8,128)(2,1)} fusion(f32[2048,384]{1,0:T(8,128)} %reduce-scatter.4.cloned.1.call-done), kind=kLoop, calls=%fused_computation.19 | loop fusion | flops 786432 | bytes 4718592 | tf_op jit(solution)/shard_map/broadcast_in_dim | solution.py:144
  212.4 3.2 %convert_bitcast_fusion.1 = bf16[1,2048,384]{2,1,0:T(8,128)(2,1)} fusion(f32[2048,384]{1,0:T(8,128)} %reduce-scatter.6.cloned.1.call-done), kind=kLoop, calls=%fused_computation.18 | loop fusion | flops 786432 | bytes 4718592 | tf_op jit(solution)/shard_map/broadcast_in_dim | solution.py:145
  (40 shorter events, 0.1 us)
Async XLA Ops:
  7.2 1.5 copy-start.16
  7.2 1.6 copy-start.17
  7.2 2.5 %copy-start.5 = (bf16[16,2048]{1,0:T(8,128)(2,1)S(1)}, bf16[16,2048]{1,0:T(8,128)(2,1)}, u32[]{:S(2)}) copy-start(bf16[16,2048]{1,0:T(8,128)(2,1)} %param.15) | copy-start | bytes 196612
  7.2 66.0 %all-gather.11.cloned.1.call-start = ((), (), s32[]{:S(2)}) async-start(), calls=%async_computation.12 | async-start | bytes 4718592 | tf_op jit(solution)/shard_map/all_gather | solution.py:90
  7.9 68.4 %all-gather.9.cloned.1.call-start = ((), (), s32[]{:S(2)}) async-start(), calls=%async_computation.11 | async-start | bytes 4718592 | tf_op jit(solution)/shard_map/all_gather | solution.py:89
  8.8 10.8 %copy-start.12 = (f32[16,8]{1,0:T(8,128)}, f32[16,8]{1,0:T(8,128)S(1)}, u32[]{:S(2)}) copy-start(f32[16,8]{1,0:T(8,128)S(1)} %copy.23) | copy-start | bytes 1540
  9.5 10.3 %copy-start.10 = (s32[16,8]{1,0:T(8,128)}, s32[16,8]{1,0:T(8,128)S(1)}, u32[]{:S(2)}) copy-start(s32[16,8]{1,0:T(8,128)S(1)} %multiply_add_fusion) | copy-start | bytes 1540
  9.5 10.1 %copy-start.6 = (bf16[16,2048]{1,0:T(8,128)(2,1)S(1)}, bf16[16,2048]{1,0:T(8,128)(2,1)}, u32[]{:S(2)}) copy-start(bf16[16,2048]{1,0:T(8,128)(2,1)} %param.8) | copy-start | bytes 196612
  9.7 10.6 %copy-start.8 = (bf16[16,176]{1,0:T(8,128)(2,1)}, bf16[16,176]{1,0:T(8,128)(2,1)S(1)}, u32[]{:S(2)}) copy-start(bf16[16,176]{1,0:T(8,128)(2,1)S(1)} %get-tuple-element.10) | copy-start | bytes 16900
  9.7 10.6 %copy-start.7 = (f32[2048]{0:T(1024)S(1)}, f32[2048]{0:T(1024)}, u32[]{:S(2)}) copy-start(f32[2048]{0:T(1024)} %param.9) | copy-start | bytes 24580
  11.7 30.8 %all-to-all-start.2 = ((bf16[16,11,2048]{2,1,0:T(8,128)(2,1)}), bf16[16,11,2048]{2,1,0:T(8,128)(2,1)S(1)}, u32[]{:S(2)}, u32[]{:S(2)}) async-start(bf16[16,11,2048]{2,1,0:T(8,128)(2,1)} %reshape.111), calls=%async_computation.2 | async-start | bytes 2097152 | tf_op jit(solution)/shard_map/all_to_all | solution.py:79
  18.9 60.1 %all-gather.7.cloned.1.call-start = ((), (), s32[]{:S(2)}) async-start(), calls=%async_computation.10 | async-start | bytes 4718592 | tf_op jit(solution)/shard_map/all_gather | solution.py:88
  20.3 22.2 %copy-start.14 = (f32[16]{0:T(128)}, f32[16]{0:T(128)S(1)}, u32[]{:S(2)}) copy-start(f32[16]{0:T(128)S(1)} %get-tuple-element.17) | copy-start | bytes 196
  42.5 30.5 %all-to-all-start = ((bf16[16,11,2048]{2,1,0:T(8,128)(2,1)}), bf16[16,11,2048]{2,1,0:T(8,128)(2,1)S(1)}, u32[]{:S(2)}, u32[]{:S(2)}) async-start(bf16[16,11,2048]{2,1,0:T(8,128)(2,1)} %reshape.107), calls=%async_computation | async-start | bytes 2097152 | tf_op jit(solution)/shard_map/all_to_all | solution.py:72
  49.9 156.0 %reduce-scatter.8.cloned.1.call-start = ((), (), s32[]{:S(2)}) async-start(), calls=%async_computation.9 | async-start | bytes 9437184 | tf_op jit(solution)/shard_map/reduce_scatter | solution.py:102
  81.8 3.7 %copy-start.2 = (bf16[176,768]{1,0:T(8,128)(2,1)}, bf16[176,768]{1,0:T(8,128)(2,1)S(1)}, u32[]{:S(2)}) copy-start(bf16[176,768]{1,0:T(8,128)(2,1)S(1)} %get-tuple-element.11) | copy-start | bytes 811012
  81.8 7.5 %copy-start.4 = (bf16[176,768]{1,0:T(8,128)(2,1)}, bf16[176,768]{1,0:T(8,128)(2,1)S(1)}, u32[]{:S(2)}) copy-start(bf16[176,768]{1,0:T(8,128)(2,1)S(1)} %get-tuple-element.12) | copy-start | bytes 811012
  85.5 123.8 %reduce-scatter.4.cloned.1.call-start = ((), (), s32[]{:S(2)}) async-start(), calls=%async_computation.7 | async-start | bytes 9437184 | tf_op jit(solution)/shard_map/reduce_scatter | solution.py:100
  89.3 123.2 %reduce-scatter.6.cloned.1.call-start = ((), (), s32[]{:S(2)}) async-start(), calls=%async_computation.8 | async-start | bytes 9437184 | tf_op jit(solution)/shard_map/reduce_scatter | solution.py:101
  93.3 15.6 %copy-start = (bf16[1,2048,768]{2,1,0:T(8,128)(2,1)S(1)}, bf16[1,2048,768]{2,1,0:T(8,128)(2,1)}, u32[]{:S(2)}) copy-start(bf16[1,2048,768]{2,1,0:T(8,128)(2,1)} %all-gather.9.cloned.1.call-done) | copy-start | bytes 9437188
  99.6 11.6 %copy-start.3 = (bf16[176,768]{1,0:T(8,128)(2,1)S(1)}, bf16[176,768]{1,0:T(8,128)(2,1)}, u32[]{:S(2)}) copy-start(bf16[176,768]{1,0:T(8,128)(2,1)} %copy-done.2) | copy-start | bytes 811012
  99.6 31.8 %all-to-all-start.1 = ((bf16[16,11,2048]{2,1,0:T(8,128)(2,1)}), bf16[16,11,2048]{2,1,0:T(8,128)(2,1)}, u32[]{:S(2)}, u32[]{:S(2)}) async-start(bf16[16,11,2048]{2,1,0:T(8,128)(2,1)} %reshape.109), calls=%async_computation.1 | async-start | bytes 2097152 | tf_op jit(solution)/shard_map/all_to_all | solution.py:107
  108.9 2.3 %copy-start.1 = (bf16[1,2048,768]{2,1,0:T(8,128)(2,1)S(1)}, bf16[1,2048,768]{2,1,0:T(8,128)(2,1)}, u32[]{:S(2)}) copy-start(bf16[1,2048,768]{2,1,0:T(8,128)(2,1)} %all-gather.7.cloned.1.call-done) | copy-start | bytes 9437188
  112.4 28.0 %copy-start.11 = (s32[16,8]{1,0:T(8,128)S(1)}, s32[16,8]{1,0:T(8,128)}, u32[]{:S(2)}) copy-start(s32[16,8]{1,0:T(8,128)} %copy-done.10) | copy-start | bytes 1540
  112.4 28.0 %copy-start.13 = (f32[16,8]{1,0:T(8,128)S(1)}, f32[16,8]{1,0:T(8,128)}, u32[]{:S(2)}) copy-start(f32[16,8]{1,0:T(8,128)} %copy-done.12) | copy-start | bytes 1540
  131.4 30.4 %all-to-all-start.3 = ((bf16[16,11,2048]{2,1,0:T(8,128)(2,1)}), bf16[16,11,2048]{2,1,0:T(8,128)(2,1)S(1)}, u32[]{:S(2)}, u32[]{:S(2)}) async-start(bf16[16,11,2048]{2,1,0:T(8,128)(2,1)} %reshape.113), calls=%async_computation.3 | async-start | bytes 2097152 | tf_op jit(solution)/shard_map/all_to_all | solution.py:114
  138.9 23.2 %copy-start.9 = (bf16[16,176]{1,0:T(8,128)(2,1)S(1)}, bf16[16,176]{1,0:T(8,128)(2,1)}, u32[]{:S(2)}) copy-start(bf16[16,176]{1,0:T(8,128)(2,1)} %copy-done.8) | copy-start | bytes 16900
  138.9 23.2 %copy-start.15 = (f32[16]{0:T(128)S(1)}, f32[16]{0:T(128)}, u32[]{:S(2)}) copy-start(f32[16]{0:T(128)} %copy-done.14) | copy-start | bytes 196
  140.4 64.8 %copy-start.18 = (f32[16]{0:T(128)S(1)}, f32[16]{0:T(128)}, u32[]{:S(2)}) copy-start(f32[16]{0:T(128)} %get-tuple-element.16) | copy-start | bytes 196
Sparse Core Ops, SparseCore 0:
  9.6 13.4 all-gather.10
  24.6 13.1 all-gather.8
  39.4 13.1 all-gather.6
  85.6 15.8 reduce-scatter.7
  103.6 15.1 reduce-scatter.3
  120.9 15.0 reduce-scatter.5
where the time goes:
time: 223 us; the launch traced here: 222 us
  waiting for transfers between devices  82.1 us (37%)
  blocking collectives  42.8 us (19%)
  starting transfers between devices  31.6 us (14%)
  matrix products  30.1 us (13%)
  between operations  14.5 us (7%)
  other arithmetic  11.7 us (5%)
  local copies, waits for them, and re-layouts  9.69 us (4%)
    psum x1, blocking collectives, local(): lax.psum(jnp.sum(d_normed * x_float * inv_rms, axis=0), ('ctx', 'grp', 's...  42.8 us
    all_to_all x1, waiting for transfers between devices, local(): lax.all_to_all(send_rows.reshape(experts, slots, width), ('ctx', 'grp'),...  22.6 us
    all_to_all x1, waiting for transfers between devices, local(): lax.all_to_all(send_grads.reshape(experts, slots, width), ('ctx', 'grp'),...  20.6 us
    all_to_all x1, waiting for transfers between devices, local(): lax.all_to_all(back_rows.reshape(experts, slots, width), ('ctx', 'grp'),...  19 us
    all_to_all x1, waiting for transfers between devices, local(): lax.all_to_all(back_out.reshape(experts, slots, width), ('ctx', 'grp'), s...  17.7 us
    all_to_all x1, starting transfers between devices, local(): lax.all_to_all(back_out.reshape(experts, slots, width), ('ctx', 'grp'), s...  9.28 us
    all_to_all x1, starting transfers between devices, local(): lax.all_to_all(back_rows.reshape(experts, slots, width), ('ctx', 'grp'),...  7.49 us
    all_to_all x1, starting transfers between devices, local(): lax.all_to_all(send_rows.reshape(experts, slots, width), ('ctx', 'grp'),...  7.48 us
  transfers between devices with their start and end apart: 10, of which 4 were waited for; matrix products, arithmetic and copies ran while one was open for 19% of the time, Pallas kernels for 0%

commit v1 on v0

--- a/solution.py
+++ b/solution.py
@@ -129,7 +129,9 @@
     d_normed = jnp.dot(
         token_map, came_rows.reshape(places, width), preferred_element_type=jnp.float32
     )
-    d_gain = lax.psum(jnp.sum(d_normed * x_float * inv_rms, axis=0), ("ctx", "grp", "side"))
+    d_gain = jnp.sum(d_normed * x_float * inv_rms, axis=0)
+    for name in (("grp", "side"), "ctx"):
+        d_gain = lax.psum(d_gain, name)
     scaled = d_normed * norm_gain
     d_tokens = (
         grad_float

time: 223 us -> 209 us (0.937)
  the two profiles are of different devices: /device:TPU:12 before, /device:TPU:0 now
where the time goes in v1:
time: 209 us; the launch traced here: 208 us
  waiting for transfers between devices  97.1 us (46%)
  matrix products  31.4 us (15%)
  blocking collectives  23.7 us (11%)
  starting transfers between devices  20.6 us (10%)
  between operations  14.5 us (7%)
  other arithmetic  11.7 us (6%)
  local copies, waits for them, and re-layouts  9.45 us (5%)
    all_to_all x1, waiting for transfers between devices, local(): lax.all_to_all(send_rows.reshape(experts, slots, width), ('ctx', 'grp'),...  26.4 us
    all_to_all x1, waiting for transfers between devices, local(): lax.all_to_all(send_grads.reshape(experts, slots, width), ('ctx', 'grp'),...  24.4 us
    psum x2, blocking collectives, local(): d_gain = lax.psum(d_gain, name)  23.7 us
    all_to_all x1, waiting for transfers between devices, local(): lax.all_to_all(back_rows.reshape(experts, slots, width), ('ctx', 'grp'),...  22.6 us
    all_to_all x1, waiting for transfers between devices, local(): lax.all_to_all(back_out.reshape(experts, slots, width), ('ctx', 'grp'), s...  21.5 us
    all_to_all x1, starting transfers between devices, local(): lax.all_to_all(send_grads.reshape(experts, slots, width), ('ctx', 'grp'),...  8.34 us
    dot_general x1, matrix products, expert_pass(): lax.dot_general(rows, d_up, (((0,), (0,)), ((), ())), preferred_element_t...  4.81 us
    all_to_all x1, starting transfers between devices, local(): lax.all_to_all(back_out.reshape(experts, slots, width), ('ctx', 'grp'), s...  4.46 us
  transfers between devices with their start and end apart: 10, of which 4 were waited for; matrix products, arithmetic and copies ran while one was open for 21% of the time, Pallas kernels for 0%

profile of v1, /device:TPU:0, one launch (start us, length us, event | category | flops | bytes accessed | tf_op | source)
XLA Modules:
  0.0 208.4 jit_solution(7806166026354713469)
XLA Ops:
  7.2 0.0 all-gather.11.cloned.1.call-start
  7.2 0.7 all-gather.11.cloned.1.call-update
  7.9 0.0 all-gather.9.cloned.1.call-start
  8.0 0.7 all-gather.9.cloned.1.call-update
  8.7 0.1 copy.23
  8.8 0.1 copy.24
  8.8 0.1 eq.49
  8.9 0.1 fusion.41
  9.0 0.2 reduce_window_sum.11
  9.2 0.2 select_reduce_fusion.1
  9.4 0.1 reduce_sum.66
  9.5 0.0 copy-start.10
  9.5 0.2 select_reduce_fusion
  9.7 0.0 copy-start.7
  9.7 0.8 convolution_convert_fusion
  10.5 1.2 reshape.111
  11.7 8.3 %all-to-all-start.2 = ((bf16[16,11,2048]{2,1,0:T(8,128)(2,1)}), bf16[16,11,2048]{2,1,0:T(8,128)(2,1)S(1)}, u32[]{:S(2)}, u32[]{:S(2)}) async-start(bf16[16,11,2048]{2,1,0:T(8,128)(2,1)} %reshape.111), calls=%async_computation.2 | async-start | bytes 2097152 | tf_op jit(solution)/shard_map/all_to_all | solution.py:79
  20.0 0.0 all-gather.7.cloned.1.call-start
  20.1 0.7 all-gather.7.cloned.1.call-update
  20.8 0.1 fusion.22
  20.9 0.6 multiply_multiply_fusion
  21.5 0.4 convolution_convert_fusion.1
  21.9 1.2 reshape.107
  23.2 24.4 %all-to-all-done.2 = bf16[16,11,2048]{2,1,0:T(8,128)(2,1)S(1)} async-done(((bf16[16,11,2048]{2,1,0:T(8,128)(2,1)}), bf16[16,11,2048]{2,1,0:T(8,128)(2,1)S(1)}, u32[]{:S(2)}, u32[]{:S(2)}) %all-to-all-start.2) | async-done | bytes 720928 | tf_op jit(solution)/shard_map/all_to_all | solution.py:79
  47.5 3.7 %all-to-all-start = ((bf16[16,11,2048]{2,1,0:T(8,128)(2,1)}), bf16[16,11,2048]{2,1,0:T(8,128)(2,1)S(1)}, u32[]{:S(2)}, u32[]{:S(2)}) async-start(bf16[16,11,2048]{2,1,0:T(8,128)(2,1)} %reshape.107), calls=%async_computation | async-start | bytes 2097152 | tf_op jit(solution)/shard_map/all_to_all | solution.py:72
  51.2 0.0 reduce-scatter.8.cloned.1.call-start
  51.2 0.3 reshape.112
  51.5 26.4 %all-to-all-done = bf16[16,11,2048]{2,1,0:T(8,128)(2,1)S(1)} async-done(((bf16[16,11,2048]{2,1,0:T(8,128)(2,1)}), bf16[16,11,2048]{2,1,0:T(8,128)(2,1)S(1)}, u32[]{:S(2)}, u32[]{:S(2)}) %all-to-all-start) | async-done | bytes 720928 | tf_op jit(solution)/shard_map/all_to_all | solution.py:72
  78.0 0.3 reshape.108
  78.3 0.0 all-gather.11.cloned.1.call-done
  78.3 3.1 %fusion = f32[176,768]{1,0:T(8,128)S(1)} fusion(bf16[176,2048]{1,0:T(8,128)(2,1)S(1)} %reshape.112, bf16[1,768,2048]{2,1,0:T(8,128)(2,1)} %all-gather.11.cloned.1.call-done), kind=kOutput, calls=%fused_computation | convolution fusion | flops 553648128 | bytes 4407296 | tf_op jit(solution)/shard_map/dot_general | solution.py:16
  81.4 0.0 all-gather.9.cloned.1.call-done
  81.4 2.6 %fusion.6 = f32[176,768]{1,0:T(8,128)S(1)} fusion(bf16[176,2048]{1,0:T(8,128)(2,1)S(1)} %reshape.108, bf16[1,2048,768]{2,1,0:T(8,128)(2,1)} %all-gather.9.cloned.1.call-done), kind=kOutput, calls=%fused_computation.6 | convolution fusion | flops 553648128 | bytes 4407296 | tf_op jit(solution)/shard_map/dot_general | solution.py:11
  84.0 0.0 all-gather.7.cloned.1.call-done
  84.1 2.8 %multiply_convert_fusion.1 = (bf16[176,768]{1,0:T(8,128)(2,1)S(1)}, bf16[176,768]{1,0:T(8,128)(2,1)S(1)}, bf16[176,768]{1,0:T(8,128)(2,1)S(1)}) fusion(f32[176,768]{1,0:T(8,128)S(1)} %fusion, f32[176,768]{1,0:T(8,128)S(1)} %fusion.6, bf16[176,2048]{1,0:T(8,128)(2,1)S(1)} %reshape.108, bf16[1,2048,768]{2,1,0:T(8,128)(2,1)} %all-gather.7.cloned.1.call-done), kind=kOutput, calls=%fused_computation.22 | convolution fusion | flops 555675648 | bytes 5758976 | tf_op jit(solution)/shard_map/dot_general | solution.py:10
  86.9 3.6 %fusion.47 = f32[768,2048]{1,0:T(8,128)} fusion(bf16[176,768]{1,0:T(8,128)(2,1)S(1)} %get-tuple-element.13, bf16[176,2048]{1,0:T(8,128)(2,1)S(1)} %reshape.112), kind=kOutput, calls=%fused_computation.66 | convolution fusion | flops 553648128 | bytes 7282688 | tf_op jit(solution)/shard_map/dot_general | solution.py:33
  90.5 0.0 reduce-scatter.8.cloned.1.call-update
  90.5 0.0 reduce-scatter.4.cloned.1.call-start
  90.6 4.0 %fusion.45 = f32[2048,768]{1,0:T(8,128)} fusion(bf16[176,2048]{1,0:T(8,128)(2,1)S(1)} %reshape.108, bf16[176,768]{1,0:T(8,128)(2,1)S(1)} %get-tuple-element.11), kind=kOutput, calls=%fused_computation.64 | convolution fusion | flops 553648128 | bytes 7282688 | tf_op jit(solution)/shard_map/dot_general | solution.py:29
  94.6 0.0 reduce-scatter.4.cloned.1.call-update
  94.6 0.0 reduce-scatter.6.cloned.1.call-start
  94.7 4.8 %fusion.46 = f32[2048,768]{1,0:T(8,128)} fusion(bf16[176,2048]{1,0:T(8,128)(2,1)S(1)} %reshape.108, bf16[176,768]{1,0:T(8,128)(2,1)S(1)} %get-tuple-element.12), kind=kOutput, calls=%fused_computation.65 | convolution fusion | flops 553648128 | bytes 7282688 | tf_op jit(solution)/shard_map/dot_general | solution.py:32
  99.5 0.0 reduce-scatter.6.cloned.1.call-update
  99.5 3.9 %fusion.15 = bf16[176,2048]{1,0:T(8,128)(2,1)} fusion(bf16[176,768]{1,0:T(8,128)(2,1)S(1)} %get-tuple-element.13, bf16[1,768,2048]{2,1,0:T(8,128)(2,1)} %all-gather.11.cloned.1.call-done), kind=kOutput, calls=%fused_computation.13 | convolution fusion | flops 554008576 | bytes 4136960 | tf_op jit(solution)/shard_map/dot_general | solution.py:15
  103.4 2.3 %reshape.109 = bf16[16,11,2048]{2,1,0:T(8,128)(2,1)} reshape(bf16[176,2048]{1,0:T(8,128)(2,1)} %fusion.15) | data formatting | bytes 1441792 | tf_op jit(solution)/shard_map/reshape | solution.py:108
  105.7 4.5 %all-to-all-start.1 = ((bf16[16,11,2048]{2,1,0:T(8,128)(2,1)}), bf16[16,11,2048]{2,1,0:T(8,128)(2,1)}, u32[]{:S(2)}, u32[]{:S(2)}) async-start(bf16[16,11,2048]{2,1,0:T(8,128)(2,1)} %reshape.109), calls=%async_computation.1 | async-start | bytes 2097152 | tf_op jit(solution)/shard_map/all_to_all | solution.py:107
  110.2 2.3 %fusion.4 = f32[176,2048]{1,0:T(8,128)S(1)} fusion(bf16[176,768]{1,0:T(8,128)(2,1)} %copy-done.4, bf16[1,2048,768]{2,1,0:T(8,128)(2,1)S(1)} %copy-done), kind=kOutput, calls=%fused_computation.4 | convolution fusion | flops 553648128 | bytes 4857856 | tf_op jit(solution)/shard_map/dot_general | solution.py:26
  112.5 1.2 fusion.18
  113.7 1.2 reshape.113
  115.0 21.5 %all-to-all-done.1 = bf16[16,11,2048]{2,1,0:T(8,128)(2,1)} async-done(((bf16[16,11,2048]{2,1,0:T(8,128)(2,1)}), bf16[16,11,2048]{2,1,0:T(8,128)(2,1)}, u32[]{:S(2)}, u32[]{:S(2)}) %all-to-all-start.1) | async-done | bytes 720928 | tf_op jit(solution)/shard_map/all_to_all | solution.py:107
  136.4 3.8 %all-to-all-start.3 = ((bf16[16,11,2048]{2,1,0:T(8,128)(2,1)}), bf16[16,11,2048]{2,1,0:T(8,128)(2,1)S(1)}, u32[]{:S(2)}, u32[]{:S(2)}) async-start(bf16[16,11,2048]{2,1,0:T(8,128)(2,1)} %reshape.113), calls=%async_computation.3 | async-start | bytes 2097152 | tf_op jit(solution)/shard_map/all_to_all | solution.py:114
  140.3 1.5 reshape.118
  141.8 0.5 multiply_reduce_fusion
  142.3 1.1 fusion.32
  143.5 0.7 copy.28
  144.2 22.6 %all-to-all-done.3 = bf16[16,11,2048]{2,1,0:T(8,128)(2,1)S(1)} async-done(((bf16[16,11,2048]{2,1,0:T(8,128)(2,1)}), bf16[16,11,2048]{2,1,0:T(8,128)(2,1)S(1)}, u32[]{:S(2)}, u32[]{:S(2)}) %all-to-all-start.3) | async-done | bytes 720928 | tf_op jit(solution)/shard_map/all_to_all | solution.py:114
  166.8 0.3 reshape.114
  167.1 0.3 fusion.31
  167.4 13.9 %psum.14 = f32[2048]{0:T(1024)S(1)} all-reduce(f32[2048]{0:T(1024)S(1)} %get-tuple-element.7), channel_id=1, replica_groups=mesh['ctx'=4,'grp'=4,'side'=2] {'grp','side'}, use_global_device_ids=true, to_apply=%region_8.9 | all-reduce | flops 2048 | bytes 16384 | tf_op jit(solution)/shard_map/psum | solution.py:134
  181.4 9.8 %psum.15 = f32[2048]{0:T(1024)} all-reduce(f32[2048]{0:T(1024)S(1)} %psum.14), channel_id=1, replica_groups=mesh['ctx'=4,'grp'=4,'side'=2] {'ctx'}, use_global_device_ids=true, to_apply=%region_9.10 | all-reduce | flops 2048 | bytes 16384 | tf_op jit(solution)/shard_map/psum | solution.py:134
  191.1 0.7 fusion.28
  191.8 3.3 %convert_bitcast_fusion = bf16[1,384,2048]{2,1,0:T(8,128)(2,1)} fusion(f32[384,2048]{1,0:T(8,128)} %reduce-scatter.8.cloned.1.call-done), kind=kLoop, calls=%fused_computation.17 | loop fusion | flops 786432 | bytes 4718592 | tf_op jit(solution)/shard_map/broadcast_in_dim | solution.py:148
  195.1 3.2 %convert_bitcast_fusion.2 = bf16[1,2048,384]{2,1,0:T(8,128)(2,1)} fusion(f32[2048,384]{1,0:T(8,128)} %reduce-scatter.4.cloned.1.call-done), kind=kLoop, calls=%fused_computation.19 | loop fusion | flops 786432 | bytes 4718592 | tf_op jit(solution)/shard_map/broadcast_in_dim | solution.py:146
  198.3 3.2 %convert_bitcast_fusion.1 = bf16[1,2048,384]{2,1,0:T(8,128)(2,1)} fusion(f32[2048,384]{1,0:T(8,128)} %reduce-scatter.6.cloned.1.call-done), kind=kLoop, calls=%fused_computation.18 | loop fusion | flops 786432 | bytes 4718592 | tf_op jit(solution)/shard_map/broadcast_in_dim | solution.py:147
  (41 shorter events, 0.1 us)
Async XLA Ops:
  7.2 1.5 copy-start.16
  7.2 1.6 copy-start.17
  7.2 2.5 %copy-start.5 = (bf16[16,2048]{1,0:T(8,128)(2,1)S(1)}, bf16[16,2048]{1,0:T(8,128)(2,1)}, u32[]{:S(2)}) copy-start(bf16[16,2048]{1,0:T(8,128)(2,1)} %param.15) | copy-start | bytes 196612
  7.2 71.1 %all-gather.11.cloned.1.call-start = ((), (), s32[]{:S(2)}) async-start(), calls=%async_computation.12 | async-start | bytes 4718592 | tf_op jit(solution)/shard_map/all_gather | solution.py:90
  7.9 73.5 %all-gather.9.cloned.1.call-start = ((), (), s32[]{:S(2)}) async-start(), calls=%async_computation.11 | async-start | bytes 4718592 | tf_op jit(solution)/shard_map/all_gather | solution.py:89
  8.8 12.0 %copy-start.12 = (f32[16,8]{1,0:T(8,128)}, f32[16,8]{1,0:T(8,128)S(1)}, u32[]{:S(2)}) copy-start(f32[16,8]{1,0:T(8,128)S(1)} %copy.23) | copy-start | bytes 1540
  9.5 11.5 %copy-start.10 = (s32[16,8]{1,0:T(8,128)}, s32[16,8]{1,0:T(8,128)S(1)}, u32[]{:S(2)}) copy-start(s32[16,8]{1,0:T(8,128)S(1)} %multiply_add_fusion) | copy-start | bytes 1540
  9.5 11.3 %copy-start.6 = (bf16[16,2048]{1,0:T(8,128)(2,1)S(1)}, bf16[16,2048]{1,0:T(8,128)(2,1)}, u32[]{:S(2)}) copy-start(bf16[16,2048]{1,0:T(8,128)(2,1)} %param.8) | copy-start | bytes 196612
  9.7 11.9 %copy-start.8 = (bf16[16,176]{1,0:T(8,128)(2,1)}, bf16[16,176]{1,0:T(8,128)(2,1)S(1)}, u32[]{:S(2)}) copy-start(bf16[16,176]{1,0:T(8,128)(2,1)S(1)} %get-tuple-element.10) | copy-start | bytes 16900
  9.7 11.8 %copy-start.7 = (f32[2048]{0:T(1024)S(1)}, f32[2048]{0:T(1024)}, u32[]{:S(2)}) copy-start(f32[2048]{0:T(1024)} %param.9) | copy-start | bytes 24580
  11.7 35.8 %all-to-all-start.2 = ((bf16[16,11,2048]{2,1,0:T(8,128)(2,1)}), bf16[16,11,2048]{2,1,0:T(8,128)(2,1)S(1)}, u32[]{:S(2)}, u32[]{:S(2)}) async-start(bf16[16,11,2048]{2,1,0:T(8,128)(2,1)} %reshape.111), calls=%async_computation.2 | async-start | bytes 2097152 | tf_op jit(solution)/shard_map/all_to_all | solution.py:79
  20.0 64.0 %all-gather.7.cloned.1.call-start = ((), (), s32[]{:S(2)}) async-start(), calls=%async_computation.10 | async-start | bytes 4718592 | tf_op jit(solution)/shard_map/all_gather | solution.py:88
  21.5 26.0 %copy-start.14 = (f32[16]{0:T(128)}, f32[16]{0:T(128)S(1)}, u32[]{:S(2)}) copy-start(f32[16]{0:T(128)S(1)} %get-tuple-element.17) | copy-start | bytes 196
  47.5 30.5 %all-to-all-start = ((bf16[16,11,2048]{2,1,0:T(8,128)(2,1)}), bf16[16,11,2048]{2,1,0:T(8,128)(2,1)S(1)}, u32[]{:S(2)}, u32[]{:S(2)}) async-start(bf16[16,11,2048]{2,1,0:T(8,128)(2,1)} %reshape.107), calls=%async_computation | async-start | bytes 2097152 | tf_op jit(solution)/shard_map/all_to_all | solution.py:72
  51.2 140.6 %reduce-scatter.8.cloned.1.call-start = ((), (), s32[]{:S(2)}) async-start(), calls=%async_computation.9 | async-start | bytes 9437184 | tf_op jit(solution)/shard_map/reduce_scatter | solution.py:102
  86.9 3.7 %copy-start.2 = (bf16[176,768]{1,0:T(8,128)(2,1)}, bf16[176,768]{1,0:T(8,128)(2,1)S(1)}, u32[]{:S(2)}) copy-start(bf16[176,768]{1,0:T(8,128)(2,1)S(1)} %get-tuple-element.11) | copy-start | bytes 811012
  86.9 7.8 %copy-start.4 = (bf16[176,768]{1,0:T(8,128)(2,1)}, bf16[176,768]{1,0:T(8,128)(2,1)S(1)}, u32[]{:S(2)}) copy-start(bf16[176,768]{1,0:T(8,128)(2,1)S(1)} %get-tuple-element.12) | copy-start | bytes 811012
  90.5 104.6 %reduce-scatter.4.cloned.1.call-start = ((), (), s32[]{:S(2)}) async-start(), calls=%async_computation.7 | async-start | bytes 9437184 | tf_op jit(solution)/shard_map/reduce_scatter | solution.py:100
  94.6 103.7 %reduce-scatter.6.cloned.1.call-start = ((), (), s32[]{:S(2)}) async-start(), calls=%async_computation.8 | async-start | bytes 9437184 | tf_op jit(solution)/shard_map/reduce_scatter | solution.py:101
  99.5 10.7 %copy-start = (bf16[1,2048,768]{2,1,0:T(8,128)(2,1)S(1)}, bf16[1,2048,768]{2,1,0:T(8,128)(2,1)}, u32[]{:S(2)}) copy-start(bf16[1,2048,768]{2,1,0:T(8,128)(2,1)} %all-gather.9.cloned.1.call-done) | copy-start | bytes 9437188
  105.7 6.8 %copy-start.3 = (bf16[176,768]{1,0:T(8,128)(2,1)S(1)}, bf16[176,768]{1,0:T(8,128)(2,1)}, u32[]{:S(2)}) copy-start(bf16[176,768]{1,0:T(8,128)(2,1)} %copy-done.2) | copy-start | bytes 811012
  105.7 30.7 %all-to-all-start.1 = ((bf16[16,11,2048]{2,1,0:T(8,128)(2,1)}), bf16[16,11,2048]{2,1,0:T(8,128)(2,1)}, u32[]{:S(2)}, u32[]{:S(2)}) async-start(bf16[16,11,2048]{2,1,0:T(8,128)(2,1)} %reshape.109), calls=%async_computation.1 | async-start | bytes 2097152 | tf_op jit(solution)/shard_map/all_to_all | solution.py:107
  110.2 2.3 %copy-start.1 = (bf16[1,2048,768]{2,1,0:T(8,128)(2,1)S(1)}, bf16[1,2048,768]{2,1,0:T(8,128)(2,1)}, u32[]{:S(2)}) copy-start(bf16[1,2048,768]{2,1,0:T(8,128)(2,1)} %all-gather.7.cloned.1.call-done) | copy-start | bytes 9437188
  113.7 28.1 %copy-start.11 = (s32[16,8]{1,0:T(8,128)S(1)}, s32[16,8]{1,0:T(8,128)}, u32[]{:S(2)}) copy-start(s32[16,8]{1,0:T(8,128)} %copy-done.10) | copy-start | bytes 1540
  113.7 28.1 %copy-start.13 = (f32[16,8]{1,0:T(8,128)S(1)}, f32[16,8]{1,0:T(8,128)}, u32[]{:S(2)}) copy-start(f32[16,8]{1,0:T(8,128)} %copy-done.12) | copy-start | bytes 1540
  136.4 30.4 %all-to-all-start.3 = ((bf16[16,11,2048]{2,1,0:T(8,128)(2,1)}), bf16[16,11,2048]{2,1,0:T(8,128)(2,1)S(1)}, u32[]{:S(2)}, u32[]{:S(2)}) async-start(bf16[16,11,2048]{2,1,0:T(8,128)(2,1)} %reshape.113), calls=%async_computation.3 | async-start | bytes 2097152 | tf_op jit(solution)/shard_map/all_to_all | solution.py:114
  140.3 26.8 %copy-start.9 = (bf16[16,176]{1,0:T(8,128)(2,1)S(1)}, bf16[16,176]{1,0:T(8,128)(2,1)}, u32[]{:S(2)}) copy-start(bf16[16,176]{1,0:T(8,128)(2,1)} %copy-done.8) | copy-start | bytes 16900
  140.3 26.8 %copy-start.15 = (f32[16]{0:T(128)S(1)}, f32[16]{0:T(128)}, u32[]{:S(2)}) copy-start(f32[16]{0:T(128)} %copy-done.14) | copy-start | bytes 196
  141.8 49.3 %copy-start.18 = (f32[16]{0:T(128)S(1)}, f32[16]{0:T(128)}, u32[]{:S(2)}) copy-start(f32[16]{0:T(128)} %get-tuple-element.16) | copy-start | bytes 196
Sparse Core Ops, SparseCore 0:
  9.6 14.8 all-gather.10
  26.0 13.1 all-gather.8
  40.8 13.1 all-gather.6
  90.6 11.2 reduce-scatter.7
  104.1 15.8 reduce-scatter.3
  122.1 15.0 reduce-scatter.5
